TPU v7x, 512 devices: a whole 4x4x16 slice. The times are simulated.
512 devices in a mesh: hx: 32 (over x, z_lo), hy: 4 (over y), vz: 4 (over z_hi, core).
Axes of the slice: x: 4, y: 4, z: 16 (z_hi: 2, z_lo: 8; z = z_hi * 8 + z_lo), core: 2. Of those that a mesh axis runs over, the one named last changes fastest.
Arguments:
- prognostic: float32 [5, 80, 4, 4, 4, 4096], P(None, 'vz', None, None, 'hy', 'hx'), may hold values from -6 to 6
- metric: float32 [4, 4, 4, 4096], P(None, None, 'hy', 'hx'), may hold values from 0.5 to 2
- first_flux: float32 [5, 5], replicated, may hold values from -2.5 to 2.5
- second_flux: float32 [5, 5], replicated, may hold values from -2.5 to 2.5
- neighbour_face: int32 [4, 4, 4096], P(None, 'hy', 'hx'), may hold values from 0 to 3
- orientation: int32 [4, 4, 4096], P(None, 'hy', 'hx'), may hold values from 0 to 1
- coupling: float32 [4, 80, 4, 4, 4, 4096], P(None, None, 'vz', None, 'hy', 'hx'), may hold values from 0.1 to 1
- damping: float32 [4, 4, 4, 4096], P('vz', None, 'hy', 'hx'), may hold values from 0.005 to 0.05
Outputs:
- updated: float32 [5, 80, 4, 4, 4, 4096], P(None, 'vz', None, None, 'hy', 'hx')
All inputs are finite; a program needn't handle non-finite values.
Results may differ from a plain program's by a relative error of at most 0.0003.
Values sent between devices are 32-bit elements; how exact they have to be, the bound alone decides.
A program may use at most 64 MiB of HBM per device.

v0:
```python
import jax
import jax.numpy as jnp
import numpy as np
from jax import lax
from jax.sharding import PartitionSpec as P

step_size = 0.05
rusanov_speed = 1.0
lift_weight = 6.0
gravity_couple = 0.5
density_couple = 0.3
theta_couple = 0.4


def extended(x, sides, width):
    for axis, dim in sides:
        size, length = (lax.axis_size(axis), x.shape[dim])
        up = [(i, (i + 1) % size) for i in range(size)]
        down = [(j, i) for i, j in up]
        last = lax.slice_in_dim(x, length - width, length, axis=dim)
        initial = lax.slice_in_dim(x, 0, width, axis=dim)
        before = lax.ppermute(last, axis, up)
        after = lax.ppermute(initial, axis, down)
        x = jnp.concatenate([before, x, after], axis=dim)
    return x


def derivative_table():
    points = np.array([-1.0, -1.0 / np.sqrt(5.0), 1.0 / np.sqrt(5.0), 1.0])
    number = points.shape[0]
    barycentric = np.ones(number)
    for source in range(number):
        for another in range(number):
            if another != source:
                barycentric[source] = barycentric[source] / (points[source] - points[another])
    matrix = np.zeros((number, number))
    for target in range(number):
        for source in range(number):
            if target != source:
                matrix[target, source] = (
                    barycentric[source] / barycentric[target] / (points[target] - points[source])
                )
        matrix[target, target] = -np.sum(matrix[target])
    return jnp.asarray(matrix, dtype=jnp.float32)


def face_traces(fields):
    west_face = fields[:, :, :, 0]
    east_face = fields[:, :, :, -1]
    south_face = fields[:, :, 0, :]
    north_face = fields[:, :, -1, :]
    return jnp.stack([west_face, east_face, south_face, north_face], axis=2)


def pick_face(candidates, table_row, flip_row):
    chosen = jnp.zeros(candidates.shape[:2] + candidates.shape[3:], candidates.dtype)
    for option in range(candidates.shape[2]):
        chosen = chosen + jnp.where(table_row == option, candidates[:, :, option], 0.0)
    reverse = chosen[:, :, ::-1]
    return jnp.where(flip_row == 1, reverse, chosen)


def section_values(fields, outer_traces, metric, first_flux, second_flux):
    derivative = derivative_table()
    highest = lax.Precision.HIGHEST
    flux_first = jnp.einsum("fg,gljiab->fljiab", first_flux, fields, precision=highest)
    flux_second = jnp.einsum("fg,gljiab->fljiab", second_flux, fields, precision=highest)
    divergence = jnp.einsum("ci,fljiab->fljcab", derivative, flux_first, precision=highest)
    divergence = divergence + jnp.einsum(
        "cj,fljiab->flciab", derivative, flux_second, precision=highest
    )
    own_traces = face_traces(fields)
    own_first = face_traces(flux_first)
    own_second = face_traces(flux_second)
    own_normal = jnp.stack(
        [-own_first[:, :, 0], own_first[:, :, 1], -own_second[:, :, 2], own_second[:, :, 3]], axis=2
    )
    outer_first = jnp.einsum(
        "fg,glhkab->flhkab", first_flux, outer_traces[:, :, 0:2], precision=highest
    )
    outer_second = jnp.einsum(
        "fg,glhkab->flhkab", second_flux, outer_traces[:, :, 2:4], precision=highest
    )
    outer_normal = jnp.concatenate(
        [
            -outer_first[:, :, 0:1],
            outer_first[:, :, 1:2],
            -outer_second[:, :, 0:1],
            outer_second[:, :, 1:2],
        ],
        axis=2,
    )
    correction = 0.5 * (own_normal - outer_normal) + 0.5 * rusanov_speed * (
        outer_traces - own_traces
    )
    blank_face = jnp.zeros_like(correction[:, :, 0])
    middle_blanks = [blank_face] * (fields.shape[3] - 2)
    across_first = jnp.stack([correction[:, :, 0]] + middle_blanks + [correction[:, :, 1]], axis=3)
    across_second = jnp.stack([correction[:, :, 2]] + middle_blanks + [correction[:, :, 3]], axis=2)
    tendency = metric * (lift_weight * (across_first + across_second) - divergence)
    return fields + step_size * tendency


def level_difference(column_values):
    upper_part = jnp.concatenate([column_values[1:], jnp.zeros_like(column_values[:1])], axis=0)
    lower_part = jnp.concatenate([jnp.zeros_like(column_values[:1]), column_values[:-1]], axis=0)
    return upper_part - lower_part


def solve_unrolled(entry_a, entry_b, centre, entry_d, entry_e, source):
    levels = source.shape[0]
    empty_row = jnp.zeros_like(source[0])
    far_ratio, far_second, far_value = (empty_row, empty_row, empty_row)
    near_ratio, near_second, near_value = (empty_row, empty_row, empty_row)
    ratios, seconds, scaled = ([], [], [])
    for height in range(levels):
        reduced = entry_b[height] - entry_a[height] * far_ratio
        pivot_entry = centre[height] - entry_a[height] * far_second - reduced * near_ratio
        upper_ratio = (entry_d[height] - reduced * near_second) / pivot_entry
        second_ratio = entry_e[height] / pivot_entry
        scaled_value = (
            source[height] - entry_a[height] * far_value - reduced * near_value
        ) / pivot_entry
        far_ratio, far_second, far_value = (near_ratio, near_second, near_value)
        near_ratio, near_second, near_value = (upper_ratio, second_ratio, scaled_value)
        ratios.append(upper_ratio)
        seconds.append(second_ratio)
        scaled.append(scaled_value)
    next_one, next_two = (empty_row, empty_row)
    solution = [None] * levels
    for height in range(levels - 1, -1, -1):
        solved = scaled[height] - ratios[height] * next_one - seconds[height] * next_two
        solution[height] = solved
        next_two, next_one = (next_one, solved)
    return jnp.stack(solution)


def per_device(
    prognostic, metric, first_flux, second_flux, neighbour_face, orientation, coupling, damping
):
    own_traces = face_traces(prognostic)
    extent_first = own_traces.shape[4]
    extent_second = own_traces.shape[5]
    padded = extended(own_traces, (("hx", 5), ("hy", 4)), 1)
    west_outer = pick_face(
        padded[..., 0:extent_first, 1 : extent_second + 1], neighbour_face[0], orientation[0]
    )
    east_outer = pick_face(
        padded[..., 2:, 1 : extent_second + 1], neighbour_face[1], orientation[1]
    )
    south_outer = pick_face(
        padded[..., 1 : extent_first + 1, 0:extent_second], neighbour_face[2], orientation[2]
    )
    north_outer = pick_face(
        padded[..., 1 : extent_first + 1, 2:], neighbour_face[3], orientation[3]
    )
    outer_traces = jnp.stack([west_outer, east_outer, south_outer, north_outer], axis=2)
    section_state = section_values(prognostic, outer_traces, metric, first_flux, second_flux)
    columns = lax.all_to_all(section_state[3:5], "vz", split_axis=2, concat_axis=1, tiled=True)
    source = columns[0] - gravity_couple * level_difference(columns[1])
    centre = coupling[0] + coupling[1] + coupling[2] + coupling[3] + damping[None]
    vertical_speed = solve_unrolled(
        -coupling[0], -coupling[1], centre, -coupling[2], -coupling[3], source
    )
    speed_jump = level_difference(vertical_speed)
    returned = lax.all_to_all(
        jnp.stack([vertical_speed, speed_jump]), "vz", split_axis=1, concat_axis=2, tiled=True
    )
    speed_here = returned[0]
    jump_here = returned[1]
    return jnp.stack(
        [
            section_state[0] - density_couple * jump_here,
            section_state[1],
            section_state[2],
            speed_here,
            section_state[4] - theta_couple * jump_here,
        ]
    )


def solution(mesh):
    placed = (
        P(None, "vz", None, None, "hy", "hx"),
        P(None, None, "hy", "hx"),
        P(),
        P(),
        P(None, "hy", "hx"),
        P(None, "hy", "hx"),
        P(None, None, "vz", None, "hy", "hx"),
        P("vz", None, "hy", "hx"),
    )
    return jax.shard_map(
        per_device,
        mesh=mesh,
        in_specs=placed,
        out_specs=P(None, "vz", None, None, "hy", "hx"),
        check_vma=False,
    )
```

profile of v0, /device:TPU:1, one launch (start us, length us, event | category | flops | bytes accessed | tf_op | source)
XLA Modules:
  0.0 184.2 jit_solution(2517463103171061723)
XLA Ops:
  0.0 1.3 fusion.1374
  1.3 1.3 fusion.1375
  3.1 1.5 fusion.1372
  4.7 2.0 %copy.1166 = f32[5,20,4,4,1,1]{1,3,5,4,2,0:T(4,128)S(1)} copy(f32[5,20,4,4,1,1]{5,0,3,1,4,2:T(8,128)} %get-tuple-element.737) | data formatting | bytes 12800 | tf_op jit(solution)/shard_map/slice | solution.py:20
  6.7 4.4 %collective-permute-start = (f32[5,20,4,4,1,1]{1,3,5,4,2,0:T(4,128)S(1)}, f32[5,20,4,4,1,1]{1,3,5,4,2,0:T(4,128)S(1)}, u32[]{:S(2)}, u32[]{:S(2)}) collective-permute-start(f32[5,20,4,4,1,1]{1,3,5,4,2,0:T(4,128)S(1)} %copy.1166), channel_id=1, source_target_pairs={{0,16},{16,32},{32,48},{48,64},{64,80},{80,96},{96,112},{112,128},... | collective-permute-start | bytes 19208 | tf_op jit(solution)/shard_map/ppermute | solution.py:22
  11.1 1.3 copy.1167
  12.4 13.6 %collective-permute-start.1 = (f32[5,20,4,4,1,1]{1,3,5,4,2,0:T(4,128)}, f32[5,20,4,4,1,1]{1,3,5,4,2,0:T(4,128)}, u32[]{:S(2)}, u32[]{:S(2)}) collective-permute-start(f32[5,20,4,4,1,1]{1,3,5,4,2,0:T(4,128)} %copy.1167), channel_id=1, source_target_pairs={{16,0},{32,16},{48,32},{64,48},{80,64},{96,80},{112,96},{128,112},... | collective-permute-start | bytes 19208 | tf_op jit(solution)/shard_map/ppermute | solution.py:23
  26.0 1.6 fusion.2
  27.7 0.9 fusion.40
  28.6 0.8 slice_bitcast_fusion.2
  30.0 1.6 fusion
  31.8 0.9 slice_negate_fusion.2
  32.7 2.9 %fusion.12 = f32[5,20,4,128,4]{3,4,2,1,0:T(4,128)} fusion(f32[4,4,1,1,1]{1,0,4,3,2:T(4,128)S(1)} %copy-done.59, f32[5,20,4,4,128]{4,0,3,2,1:T(8,128)S(1)} %fusion), kind=kOutput, calls=%fused_computation.22 | convolution fusion | flops 9830400 | bytes 1638464 | tf_op jit(solution)/shard_map/cj,fljiab->flciab/dot_general | solution.py:69
  35.6 0.9 slice_negate_fusion.4
  37.7 2.4 %copy.1168 = f32[5,20,4,4,1,1]{5,0,3,1,4,2:T(8,128)} copy(f32[5,20,4,4,1,1]{1,3,5,4,2,0:T(4,128)S(1)} %collective-permute-done) | data formatting | bytes 12800 | tf_op jit(solution)/shard_map/ppermute | solution.py:22
  40.1 2.2 %copy.1169 = f32[5,20,4,4,1,1]{5,0,3,1,4,2:T(8,128)S(1)} copy(f32[5,20,4,4,1,1]{1,3,5,4,2,0:T(4,128)} %collective-permute-done.1) | data formatting | bytes 12800 | tf_op jit(solution)/shard_map/ppermute | solution.py:23
  42.2 2.4 %pad_maximum_fusion = f32[5,20,4,4,1,130]{5,0,3,1,4,2:T(8,128)S(1)} fusion(f32[5,20,4,4,1,1]{5,0,3,1,4,2:T(8,128)S(1)} %copy.1169, f32[5,20,1,4,1,128]{5,0,3,1,4,2:T(8,128)S(1)} %copy.1567, f32[5,20,1,4,1,128]{5,0,3,1,4,2:T(8,128)S(1)} %copy.1566, f32[5,20,1,4,1,128]{5,0,3,1,4,2:T(8,128)S(1)} %get-tuple-element.861, ...), kind=kLoop, calls=%fused_computation | loop fusion | flops 1040000 | bytes 1664000 | tf_op jit(solution)/shard_map/concatenate | solution.py:24
  45.4 3.2 %collective-permute-start.2 = (f32[5,20,4,4,1,130]{5,3,4,2,1,0:T(4,128)S(1)}, f32[5,20,4,4,1,130]{5,3,4,2,1,0:T(4,128)S(1)}, u32[]{:S(2)}, u32[]{:S(2)}) collective-permute-start(f32[5,20,4,4,1,130]{5,3,4,2,1,0:T(4,128)S(1)} %copy.1170), channel_id=1, source_target_pairs={{0,4},{4,8},{8,12},{12,0},{1,5},{5,9},{9,13},{13,1},{2,6},{6,10},{... | collective-permute-start | bytes 2496008 | tf_op jit(solution)/shard_map/ppermute | solution.py:22
  48.6 3.6 %collective-permute-start.3 = (f32[5,20,4,4,1,130]{5,3,4,2,1,0:T(4,128)S(1)}, f32[5,20,4,4,1,130]{5,3,4,2,1,0:T(4,128)S(1)}, u32[]{:S(2)}, u32[]{:S(2)}) collective-permute-start(f32[5,20,4,4,1,130]{5,3,4,2,1,0:T(4,128)S(1)} %copy.1170), channel_id=1, source_target_pairs={{4,0},{8,4},{12,8},{0,12},{5,1},{9,5},{13,9},{1,13},{6,2},{10,6},{... | collective-permute-start | bytes 2496008 | tf_op jit(solution)/shard_map/ppermute | solution.py:23
  54.6 27.8 %collective-permute-done.2 = f32[5,20,4,4,1,130]{5,3,4,2,1,0:T(4,128)S(1)} collective-permute-done((f32[5,20,4,4,1,130]{5,3,4,2,1,0:T(4,128)S(1)}, f32[5,20,4,4,1,130]{5,3,4,2,1,0:T(4,128)S(1)}, u32[]{:S(2)}, u32[]{:S(2)}) %collective-permute-start.2) | collective-permute-done | bytes 832032 | tf_op jit(solution)/shard_map/ppermute | solution.py:22
  83.3 2.2 %collective-permute-done.3 = f32[5,20,4,4,1,130]{5,3,4,2,1,0:T(4,128)S(1)} collective-permute-done((f32[5,20,4,4,1,130]{5,3,4,2,1,0:T(4,128)S(1)}, f32[5,20,4,4,1,130]{5,3,4,2,1,0:T(4,128)S(1)}, u32[]{:S(2)}, u32[]{:S(2)}) %collective-permute-start.3) | collective-permute-done | bytes 832032 | tf_op jit(solution)/shard_map/ppermute | solution.py:23
  90.0 2.3 %fusion.10 = f32[5,20,4,4,1,128]{5,3,2,1,0,4:T(4,128)S(1)} fusion(f32[5,20,4,4,1,128]{5,3,2,1,0,4:T(4,128)S(1)} %bitcast.7058, f32[4,4,1,1,1]{1,0,4,3,2:T(4,128)S(1)} %copy-done.59, f32[5,20,4,1,1,128]{5,3,2,1,0,4:T(1,128)S(1)} %copy.1183, f32[5,20,4,1,1,128]{5,3,2,1,0,4:T(1,128)S(1)} %copy.1182, f32[5,20,1,4,1,128]{5,3,2,1,0,4:T(4,128)S(1)} %copy.1185, ...), kind=kOutput, calls=%fused_computation.18 | convolution fusion | flops 12083200 | bytes 4104272 | tf_op jit(solution)/shard_map/ci,fljiab->fljcab/dot_general | solution.py:68
  92.5 0.8 copy.1191
  93.2 15.2 %all-to-all-start = ((f32[2,20,4,4,1,128]{5,3,1,0,4,2:T(4,128)}), f32[2,20,4,4,1,128]{5,3,1,0,4,2:T(4,128)S(1)}, u32[]{:S(2)}, u32[]{:S(2)}) async-start(f32[2,20,4,4,1,128]{5,3,1,0,4,2:T(4,128)} %copy.1191), calls=%async_computation | async-start | bytes 655360 | tf_op jit(solution)/shard_map/all_to_all | solution.py:159
  109.3 0.8 fusion.786
  110.0 0.8 bitcast_subtract_fusion.242
  110.9 0.9 bitcast_subtract_fusion.173
  111.8 11.1 %all-to-all-done = f32[2,20,4,4,1,128]{5,3,1,0,4,2:T(4,128)S(1)} async-done(((f32[2,20,4,4,1,128]{5,3,1,0,4,2:T(4,128)}), f32[2,20,4,4,1,128]{5,3,1,0,4,2:T(4,128)S(1)}, u32[]{:S(2)}, u32[]{:S(2)}) %all-to-all-start) | async-done | bytes 327712 | tf_op jit(solution)/shard_map/all_to_all | solution.py:159
  123.4 0.8 fusion.407
  124.1 0.8 fusion.400
  124.9 0.8 fusion.393
  125.6 0.7 fusion.386
  128.6 0.8 fusion.358
  129.4 0.8 fusion.351
  130.9 0.8 fusion.337
  131.6 0.8 fusion.330
  132.4 0.8 fusion.323
  133.5 0.8 fusion.316
  134.3 0.7 fusion.309
  135.0 0.8 fusion.302
  135.8 0.9 bitcast_subtract_fusion.54
  136.7 1.1 fusion.87
  137.8 1.2 bitcast_multiply_fusion.2
  145.7 1.7 fusion.545
  147.5 0.9 multiply_subtract_fusion.109
  155.6 1.2 multiply_subtract_fusion.50
  158.1 24.8 %all_to_all.30 = f32[2,80,1,4,1,128]{5,3,4,2,0,1:T(4,128)S(1)} all-to-all(f32[2,80,1,4,1,128]{5,3,4,2,0,1:T(4,128)S(1)} %copy.1550), channel_id=1, replica_groups=mesh['hx'=32,'hy'=4,'vz'=4] {'vz'}, dimensions={1} | all-to-all | bytes 655360 | tf_op jit(solution)/shard_map/all_to_all | solution.py:166
  183.1 1.1 pad_maximum_fusion.2
  (256 shorter events, 29.7 us)
Async XLA Ops:
  0.0 30.0 %copy-start = (f32[5,5]{1,0:T(8,128)S(1)}, f32[5,5]{1,0:T(8,128)}, u32[]{:S(2)}) copy-start(f32[5,5]{1,0:T(8,128)} %param.12) | copy-start | bytes 304
  4.7 21.3 %copy-start.1 = (f32[5,20,4,4,1,128]{5,4,3,2,1,0:T(1,128)S(1)}, f32[5,20,4,4,1,128]{5,4,3,2,1,0:T(1,128)}, u32[]{:S(2)}) copy-start(f32[5,20,4,4,1,128]{5,4,3,2,1,0:T(1,128)} %param.9) | copy-start | bytes 2457604
  4.7 21.3 %copy-start.17 = (f32[5,5]{1,0:T(8,128)S(1)}, f32[5,5]{1,0:T(8,128)}, u32[]{:S(2)}) copy-start(f32[5,5]{1,0:T(8,128)} %param.11) | copy-start | bytes 304
  6.7 31.0 %collective-permute-start = (f32[5,20,4,4,1,1]{1,3,5,4,2,0:T(4,128)S(1)}, f32[5,20,4,4,1,1]{1,3,5,4,2,0:T(4,128)S(1)}, u32[]{:S(2)}, u32[]{:S(2)}) collective-permute-start(f32[5,20,4,4,1,1]{1,3,5,4,2,0:T(4,128)S(1)} %copy.1166), channel_id=1, source_target_pairs={{0,16},{16,32},{32,48},{48,64},{64,80},{80,96},{96,112},{112,128},... | collective-permute-start | bytes 19208 | tf_op jit(solution)/shard_map/ppermute | solution.py:22
  12.4 27.7 %collective-permute-start.1 = (f32[5,20,4,4,1,1]{1,3,5,4,2,0:T(4,128)}, f32[5,20,4,4,1,1]{1,3,5,4,2,0:T(4,128)}, u32[]{:S(2)}, u32[]{:S(2)}) collective-permute-start(f32[5,20,4,4,1,1]{1,3,5,4,2,0:T(4,128)} %copy.1167), channel_id=1, source_target_pairs={{16,0},{32,16},{48,32},{64,48},{80,64},{96,80},{112,96},{128,112},... | collective-permute-start | bytes 19208 | tf_op jit(solution)/shard_map/ppermute | solution.py:23
  45.4 37.0 %collective-permute-start.2 = (f32[5,20,4,4,1,130]{5,3,4,2,1,0:T(4,128)S(1)}, f32[5,20,4,4,1,130]{5,3,4,2,1,0:T(4,128)S(1)}, u32[]{:S(2)}, u32[]{:S(2)}) collective-permute-start(f32[5,20,4,4,1,130]{5,3,4,2,1,0:T(4,128)S(1)} %copy.1170), channel_id=1, source_target_pairs={{0,4},{4,8},{8,12},{12,0},{1,5},{5,9},{9,13},{13,1},{2,6},{6,10},{... | collective-permute-start | bytes 2496008 | tf_op jit(solution)/shard_map/ppermute | solution.py:22
  48.6 36.9 %collective-permute-start.3 = (f32[5,20,4,4,1,130]{5,3,4,2,1,0:T(4,128)S(1)}, f32[5,20,4,4,1,130]{5,3,4,2,1,0:T(4,128)S(1)}, u32[]{:S(2)}, u32[]{:S(2)}) collective-permute-start(f32[5,20,4,4,1,130]{5,3,4,2,1,0:T(4,128)S(1)} %copy.1170), channel_id=1, source_target_pairs={{4,0},{8,4},{12,8},{0,12},{5,1},{9,5},{13,9},{1,13},{6,2},{10,6},{... | collective-permute-start | bytes 2496008 | tf_op jit(solution)/shard_map/ppermute | solution.py:23
  54.5 28.4 %copy-start.60 = (pred[128]{0:T(512)(128)(4,1)S(1)}, pred[128]{0:T(512)(128)(4,1)}, u32[]{:S(2)}) copy-start(pred[128]{0:T(512)(128)(4,1)} %get-tuple-element.845) | copy-start | bytes 388
  54.5 28.4 %copy-start.61 = (pred[128]{0:T(512)(128)(4,1)S(1)}, pred[128]{0:T(512)(128)(4,1)}, u32[]{:S(2)}) copy-start(pred[128]{0:T(512)(128)(4,1)} %get-tuple-element.846) | copy-start | bytes 388
  54.5 28.4 %copy-start.62 = (pred[128]{0:T(512)(128)(4,1)S(1)}, pred[128]{0:T(512)(128)(4,1)}, u32[]{:S(2)}) copy-start(pred[128]{0:T(512)(128)(4,1)} %get-tuple-element.847) | copy-start | bytes 388
  54.6 28.7 %copy-start.74 = (pred[128]{0:T(512)(128)(4,1)S(1)}, pred[128]{0:T(512)(128)(4,1)}, u32[]{:S(2)}) copy-start(pred[128]{0:T(512)(128)(4,1)} %get-tuple-element.840) | copy-start | bytes 388
  92.3 16.2 %copy-start.8 = (f32[4,80,1,4,1,128]{5,4,3,2,1,0:T(1,128)S(1)}, f32[4,80,1,4,1,128]{5,4,3,2,1,0:T(1,128)}, u32[]{:S(2)}) copy-start(f32[4,80,1,4,1,128]{5,4,3,2,1,0:T(1,128)} %param.15) | copy-start | bytes 1966084
  92.3 16.1 %copy-start.58 = (f32[1,4,1,128]{3,2,1,0:T(1,128)S(1)}, f32[1,4,1,128]{3,2,1,0:T(1,128)}, u32[]{:S(2)}) copy-start(f32[1,4,1,128]{3,2,1,0:T(1,128)} %param.16) | copy-start | bytes 6148
  92.4 16.2 %copy-start.3 = (f32[1,80,1,4,1,128]{5,3,4,2,1,0:T(4,128)S(1)}, f32[1,80,1,4,1,128]{5,3,4,2,1,0:T(4,128)}, u32[]{:S(2)}) copy-start(f32[1,80,1,4,1,128]{5,3,4,2,1,0:T(4,128)} %get-tuple-element.750) | copy-start | bytes 491524
  92.4 16.2 %copy-start.4 = (f32[1,80,1,4,1,128]{5,3,4,2,1,0:T(4,128)S(1)}, f32[1,80,1,4,1,128]{5,3,4,2,1,0:T(4,128)}, u32[]{:S(2)}) copy-start(f32[1,80,1,4,1,128]{5,3,4,2,1,0:T(4,128)} %get-tuple-element.748) | copy-start | bytes 491524
  92.4 16.2 %copy-start.9 = (f32[1,80,1,4,1,128]{5,3,4,2,1,0:T(4,128)S(1)}, f32[1,80,1,4,1,128]{5,3,4,2,1,0:T(4,128)}, u32[]{:S(2)}) copy-start(f32[1,80,1,4,1,128]{5,3,4,2,1,0:T(4,128)} %get-tuple-element.749) | copy-start | bytes 491524
  92.4 16.2 %copy-start.10 = (f32[1,80,1,4,1,128]{5,3,4,2,1,0:T(4,128)S(1)}, f32[1,80,1,4,1,128]{5,3,4,2,1,0:T(4,128)}, u32[]{:S(2)}) copy-start(f32[1,80,1,4,1,128]{5,3,4,2,1,0:T(4,128)} %get-tuple-element.747) | copy-start | bytes 491524
  93.2 29.7 %all-to-all-start = ((f32[2,20,4,4,1,128]{5,3,1,0,4,2:T(4,128)}), f32[2,20,4,4,1,128]{5,3,1,0,4,2:T(4,128)S(1)}, u32[]{:S(2)}, u32[]{:S(2)}) async-start(f32[2,20,4,4,1,128]{5,3,1,0,4,2:T(4,128)} %copy.1191), calls=%async_computation | async-start | bytes 655360 | tf_op jit(solution)/shard_map/all_to_all | solution.py:159
  108.6 14.8 %copy-start.11 = (f32[80,1,4,1,128]{4,2,3,1,0:T(4,128)}, f32[80,1,4,1,128]{4,2,3,1,0:T(4,128)S(1)}, u32[]{:S(2)}) copy-start(f32[80,1,4,1,128]{4,2,3,1,0:T(4,128)S(1)} %bitcast_add_fusion) | copy-start | bytes 491524
  133.1 12.2 %copy-start.18 = (f32[4,128]{1,0:T(4,128)S(1)}, f32[4,128]{1,0:T(4,128)}, u32[]{:S(2)}) copy-start(f32[4,128]{1,0:T(4,128)} %get-tuple-element.692) | copy-start | bytes 6148
  133.1 12.2 %copy-start.19 = (f32[4,128]{1,0:T(4,128)S(1)}, f32[4,128]{1,0:T(4,128)}, u32[]{:S(2)}) copy-start(f32[4,128]{1,0:T(4,128)} %get-tuple-element.693) | copy-start | bytes 6148
  133.2 12.2 %copy-start.20 = (f32[4,128]{1,0:T(4,128)S(1)}, f32[4,128]{1,0:T(4,128)}, u32[]{:S(2)}) copy-start(f32[4,128]{1,0:T(4,128)} %get-tuple-element.698) | copy-start | bytes 6148
  133.2 12.2 %copy-start.21 = (f32[4,128]{1,0:T(4,128)S(1)}, f32[4,128]{1,0:T(4,128)}, u32[]{:S(2)}) copy-start(f32[4,128]{1,0:T(4,128)} %get-tuple-element.699) | copy-start | bytes 6148
  133.2 12.2 %copy-start.22 = (f32[4,128]{1,0:T(4,128)S(1)}, f32[4,128]{1,0:T(4,128)}, u32[]{:S(2)}) copy-start(f32[4,128]{1,0:T(4,128)} %get-tuple-element.704) | copy-start | bytes 6148
  133.2 12.2 %copy-start.23 = (f32[4,128]{1,0:T(4,128)S(1)}, f32[4,128]{1,0:T(4,128)}, u32[]{:S(2)}) copy-start(f32[4,128]{1,0:T(4,128)} %get-tuple-element.705) | copy-start | bytes 6148
  133.2 12.2 %copy-start.24 = (f32[4,128]{1,0:T(4,128)S(1)}, f32[4,128]{1,0:T(4,128)}, u32[]{:S(2)}) copy-start(f32[4,128]{1,0:T(4,128)} %get-tuple-element.573) | copy-start | bytes 6148
  133.2 12.2 %copy-start.25 = (f32[4,128]{1,0:T(4,128)S(1)}, f32[4,128]{1,0:T(4,128)}, u32[]{:S(2)}) copy-start(f32[4,128]{1,0:T(4,128)} %get-tuple-element.574) | copy-start | bytes 6148
  133.2 12.2 %copy-start.26 = (f32[4,128]{1,0:T(4,128)S(1)}, f32[4,128]{1,0:T(4,128)}, u32[]{:S(2)}) copy-start(f32[4,128]{1,0:T(4,128)} %get-tuple-element.579) | copy-start | bytes 6148
  133.2 12.2 %copy-start.27 = (f32[4,128]{1,0:T(4,128)S(1)}, f32[4,128]{1,0:T(4,128)}, u32[]{:S(2)}) copy-start(f32[4,128]{1,0:T(4,128)} %get-tuple-element.580) | copy-start | bytes 6148
  133.2 12.2 %copy-start.28 = (f32[4,128]{1,0:T(4,128)S(1)}, f32[4,128]{1,0:T(4,128)}, u32[]{:S(2)}) copy-start(f32[4,128]{1,0:T(4,128)} %get-tuple-element.585) | copy-start | bytes 6148
  133.2 12.2 %copy-start.29 = (f32[4,128]{1,0:T(4,128)S(1)}, f32[4,128]{1,0:T(4,128)}, u32[]{:S(2)}) copy-start(f32[4,128]{1,0:T(4,128)} %get-tuple-element.586) | copy-start | bytes 6148
  133.3 12.2 %copy-start.30 = (f32[4,128]{1,0:T(4,128)S(1)}, f32[4,128]{1,0:T(4,128)}, u32[]{:S(2)}) copy-start(f32[4,128]{1,0:T(4,128)} %get-tuple-element.591) | copy-start | bytes 6148
  133.3 12.2 %copy-start.31 = (f32[4,128]{1,0:T(4,128)S(1)}, f32[4,128]{1,0:T(4,128)}, u32[]{:S(2)}) copy-start(f32[4,128]{1,0:T(4,128)} %get-tuple-element.592) | copy-start | bytes 6148
  133.3 12.2 %copy-start.32 = (f32[4,128]{1,0:T(4,128)S(1)}, f32[4,128]{1,0:T(4,128)}, u32[]{:S(2)}) copy-start(f32[4,128]{1,0:T(4,128)} %get-tuple-element.597) | copy-start | bytes 6148
  133.3 12.2 %copy-start.33 = (f32[4,128]{1,0:T(4,128)S(1)}, f32[4,128]{1,0:T(4,128)}, u32[]{:S(2)}) copy-start(f32[4,128]{1,0:T(4,128)} %get-tuple-element.598) | copy-start | bytes 6148
  133.3 12.2 %copy-start.34 = (f32[4,128]{1,0:T(4,128)S(1)}, f32[4,128]{1,0:T(4,128)}, u32[]{:S(2)}) copy-start(f32[4,128]{1,0:T(4,128)} %get-tuple-element.603) | copy-start | bytes 6148
  133.3 12.2 %copy-start.35 = (f32[4,128]{1,0:T(4,128)S(1)}, f32[4,128]{1,0:T(4,128)}, u32[]{:S(2)}) copy-start(f32[4,128]{1,0:T(4,128)} %get-tuple-element.604) | copy-start | bytes 6148
  133.3 12.2 %copy-start.36 = (f32[4,128]{1,0:T(4,128)S(1)}, f32[4,128]{1,0:T(4,128)}, u32[]{:S(2)}) copy-start(f32[4,128]{1,0:T(4,128)} %get-tuple-element.609) | copy-start | bytes 6148
  133.3 12.2 %copy-start.37 = (f32[4,128]{1,0:T(4,128)S(1)}, f32[4,128]{1,0:T(4,128)}, u32[]{:S(2)}) copy-start(f32[4,128]{1,0:T(4,128)} %get-tuple-element.610) | copy-start | bytes 6148
  133.3 12.2 %copy-start.38 = (f32[4,128]{1,0:T(4,128)S(1)}, f32[4,128]{1,0:T(4,128)}, u32[]{:S(2)}) copy-start(f32[4,128]{1,0:T(4,128)} %get-tuple-element.615) | copy-start | bytes 6148
  133.3 12.2 %copy-start.39 = (f32[4,128]{1,0:T(4,128)S(1)}, f32[4,128]{1,0:T(4,128)}, u32[]{:S(2)}) copy-start(f32[4,128]{1,0:T(4,128)} %get-tuple-element.616) | copy-start | bytes 6148
  133.4 12.2 %copy-start.40 = (f32[4,128]{1,0:T(4,128)S(1)}, f32[4,128]{1,0:T(4,128)}, u32[]{:S(2)}) copy-start(f32[4,128]{1,0:T(4,128)} %get-tuple-element.621) | copy-start | bytes 6148
  133.4 12.2 %copy-start.41 = (f32[4,128]{1,0:T(4,128)S(1)}, f32[4,128]{1,0:T(4,128)}, u32[]{:S(2)}) copy-start(f32[4,128]{1,0:T(4,128)} %get-tuple-element.622) | copy-start | bytes 6148
  133.4 12.2 %copy-start.42 = (f32[4,128]{1,0:T(4,128)S(1)}, f32[4,128]{1,0:T(4,128)}, u32[]{:S(2)}) copy-start(f32[4,128]{1,0:T(4,128)} %get-tuple-element.627) | copy-start | bytes 6148
  133.4 12.2 %copy-start.43 = (f32[4,128]{1,0:T(4,128)S(1)}, f32[4,128]{1,0:T(4,128)}, u32[]{:S(2)}) copy-start(f32[4,128]{1,0:T(4,128)} %get-tuple-element.628) | copy-start | bytes 6148
  133.4 12.2 %copy-start.44 = (f32[4,128]{1,0:T(4,128)S(1)}, f32[4,128]{1,0:T(4,128)}, u32[]{:S(2)}) copy-start(f32[4,128]{1,0:T(4,128)} %get-tuple-element.633) | copy-start | bytes 6148
  133.4 12.2 %copy-start.45 = (f32[4,128]{1,0:T(4,128)S(1)}, f32[4,128]{1,0:T(4,128)}, u32[]{:S(2)}) copy-start(f32[4,128]{1,0:T(4,128)} %get-tuple-element.634) | copy-start | bytes 6148
  133.4 12.2 %copy-start.46 = (f32[4,128]{1,0:T(4,128)S(1)}, f32[4,128]{1,0:T(4,128)}, u32[]{:S(2)}) copy-start(f32[4,128]{1,0:T(4,128)} %get-tuple-element.860) | copy-start | bytes 6148
  (36 other events, 201.3 us)
where the time goes:
time: 186 us; the launch traced here: 184 us
  other arithmetic  46.4 us (25%)
  waiting for transfers between devices  41.2 us (22%)
  starting transfers between devices  40 us (22%)
  blocking collectives  24.8 us (13%)
  local copies, waits for them, and re-layouts  20.3 us (11%)
  matrix products  9.88 us (5%)
    ppermute x2, waiting for transfers between devices, extended(): before = lax.ppermute(last, axis, up)  27.8 us
    all_to_all x1, blocking collectives, per_device(): lax.all_to_all(jnp.stack([vertical_speed, speed_jump]), 'vz', split_axis=...  24.8 us
    ppermute x2, starting transfers between devices, extended(): after = lax.ppermute(initial, axis, down)  17.2 us
    all_to_all x1, starting transfers between devices, per_device(): lax.all_to_all(section_state[3:5], 'vz', split_axis=2, concat_axis=1, til...  15.2 us
    sub x34, other arithmetic, solve_unrolled(): scaled[height] - ratios[height] * next_one - seconds[height] * next_two  14.2 us
    div x21, other arithmetic, solve_unrolled(): (source[height] - entry_a[height] * far_value - reduced * near_value) / p...  13.8 us
    all_to_all x1, waiting for transfers between devices, per_device(): lax.all_to_all(section_state[3:5], 'vz', split_axis=2, concat_axis=1, til...  11.1 us
    ppermute x2, starting transfers between devices, extended(): before = lax.ppermute(last, axis, up)  7.56 us
  transfers between devices with their start and end apart: 5, of which 3 were waited for; matrix products, arithmetic and copies ran while one was open for 12% of the time, Pallas kernels for 0%

commit v1 on v0

--- a/solution.py
+++ b/solution.py
@@ -156,7 +156,12 @@
     )
     outer_traces = jnp.stack([west_outer, east_outer, south_outer, north_outer], axis=2)
     section_state = section_values(prognostic, outer_traces, metric, first_flux, second_flux)
-    columns = lax.all_to_all(section_state[3:5], "vz", split_axis=2, concat_axis=1, tiled=True)
+    columns = jnp.concatenate(
+        lax.all_to_all(
+            jnp.stack(jnp.split(section_state[3:5], lax.axis_size("vz"), axis=2)), "vz", 0, 0
+        ),
+        axis=1,
+    )
     source = columns[0] - gravity_couple * level_difference(columns[1])
     centre = coupling[0] + coupling[1] + coupling[2] + coupling[3] + damping[None]
     vertical_speed = solve_unrolled(

time: 186 us -> 179 us (0.962)
  blocking collectives: 24.8 us -> 0 us
  waiting for transfers between devices: 41.2 us -> 58.8 us
  starting transfers between devices: 40 us -> 50.4 us
  other arithmetic: 46.4 us -> 39.8 us
  local copies, waits for them, and re-layouts: 20.3 us -> 18 us
    all_to_all x1 -> x0, blocking collectives: 24.8 us -> none  [per_device(): lax.all_to_all(jnp.stack([vertical_speed, speed_jump]), 'vz', split_axis=...]
    all_to_all x1 -> x2, waiting for transfers between devices: 11.1 us -> 28.6 us  [the longest x1 14.4 us: per_device(): lax.all_to_all(jnp.stack([vertical_speed, speed_jump]), 'vz', split_axis=...]
    all_to_all x1 -> x2, starting transfers between devices: 15.2 us -> 25.6 us  [the longest x1 15.3 us: per_device(): lax.all_to_all(jnp.stack(jnp.split(section_state[3:5], lax.axis_size('vz'...]
    sub x34 -> x19, other arithmetic: 14.2 us -> 7.92 us  [solve_unrolled(): scaled[height] - ratios[height] * next_one - seconds[height] * next_two]
    mul x4 -> x0, other arithmetic: 2.54 us -> none  [the longest x1 1.17 us: solve_unrolled(): entry_a[height] * far_value]
    div x21 -> x22, other arithmetic: 13.8 us -> 15.2 us  [solve_unrolled(): (source[height] - entry_a[height] * far_value - reduced * near_value) / p...]
  transfers between devices with their start and end apart: 5 -> 6, of which waited for: 3 -> 4; matrix products, arithmetic and copies ran while one was open for 12% -> 10% of each run, Pallas kernels for 0% -> 0%
where the time goes in v1:
time: 179 us; the launch traced here: 178 us
  waiting for transfers between devices  58.8 us (33%)
  starting transfers between devices  50.4 us (28%)
  other arithmetic  39.8 us (22%)
  local copies, waits for them, and re-layouts  18 us (10%)
  matrix products  9.87 us (6%)
    ppermute x2, waiting for transfers between devices, extended(): before = lax.ppermute(last, axis, up)  27.9 us
    ppermute x2, starting transfers between devices, extended(): after = lax.ppermute(initial, axis, down)  17.2 us
    all_to_all x1, starting transfers between devices, per_device(): lax.all_to_all(jnp.stack(jnp.split(section_state[3:5], lax.axis_size('vz'...  15.3 us
    div x22, other arithmetic, solve_unrolled(): (source[height] - entry_a[height] * far_value - reduced * near_value) / p...  15.2 us
    all_to_all x1, waiting for transfers between devices, per_device(): lax.all_to_all(jnp.stack([vertical_speed, speed_jump]), 'vz', split_axis=...  14.4 us
    all_to_all x1, waiting for transfers between devices, per_device(): lax.all_to_all(jnp.stack(jnp.split(section_state[3:5], lax.axis_size('vz'...  14.1 us
    all_to_all x1, starting transfers between devices, per_device(): lax.all_to_all(jnp.stack([vertical_speed, speed_jump]), 'vz', split_axis=...  10.4 us
    sub x19, other arithmetic, solve_unrolled(): scaled[height] - ratios[height] * next_one - seconds[height] * next_two  7.92 us
  transfers between devices with their start and end apart: 6, of which 4 were waited for; matrix products, arithmetic and copies ran while one was open for 10% of the time, Pallas kernels for 0%

profile of v1, /device:TPU:1, one launch (start us, length us, event | category | flops | bytes accessed | tf_op | source)
XLA Modules:
  0.0 177.9 jit_solution(3143081680801476)
XLA Ops:
  0.0 1.3 fusion.1356
  1.3 1.3 fusion.1357
  3.1 1.5 fusion.1355
  4.7 2.0 %copy.789 = f32[5,20,4,4,1,1]{1,3,5,4,2,0:T(4,128)S(1)} copy(f32[5,20,4,4,1,1]{5,0,3,1,4,2:T(8,128)} %get-tuple-element.704) | data formatting | bytes 12800 | tf_op jit(solution)/shard_map/slice | solution.py:20
  6.7 4.4 %collective-permute-start = (f32[5,20,4,4,1,1]{1,3,5,4,2,0:T(4,128)S(1)}, f32[5,20,4,4,1,1]{1,3,5,4,2,0:T(4,128)S(1)}, u32[]{:S(2)}, u32[]{:S(2)}) collective-permute-start(f32[5,20,4,4,1,1]{1,3,5,4,2,0:T(4,128)S(1)} %copy.789), channel_id=1, source_target_pairs={{0,16},{16,32},{32,48},{48,64},{64,80},{80,96},{96,112},{112,128},... | collective-permute-start | bytes 19208 | tf_op jit(solution)/shard_map/ppermute | solution.py:22
  11.0 1.3 copy.790
  12.4 13.6 %collective-permute-start.1 = (f32[5,20,4,4,1,1]{1,3,5,4,2,0:T(4,128)}, f32[5,20,4,4,1,1]{1,3,5,4,2,0:T(4,128)S(1)}, u32[]{:S(2)}, u32[]{:S(2)}) collective-permute-start(f32[5,20,4,4,1,1]{1,3,5,4,2,0:T(4,128)} %copy.790), channel_id=1, source_target_pairs={{16,0},{32,16},{48,32},{64,48},{80,64},{96,80},{112,96},{128,112},... | collective-permute-start | bytes 19208 | tf_op jit(solution)/shard_map/ppermute | solution.py:23
  26.0 1.6 fusion.2
  27.7 0.9 fusion.40
  28.6 0.8 slice_bitcast_fusion.2
  29.9 1.6 fusion
  31.7 0.9 slice_negate_fusion.2
  32.6 2.9 %fusion.12 = f32[5,20,4,128,4]{3,4,2,1,0:T(4,128)} fusion(f32[4,4,1,1,1]{1,0,4,3,2:T(4,128)S(1)} %copy-done.22, f32[5,20,4,4,128]{4,0,3,2,1:T(8,128)S(1)} %fusion), kind=kOutput, calls=%fused_computation.22 | convolution fusion | flops 9830400 | bytes 1638464 | tf_op jit(solution)/shard_map/cj,fljiab->flciab/dot_general | solution.py:69
  36.6 2.4 %copy.791 = f32[5,20,4,4,1,1]{5,0,3,1,4,2:T(8,128)} copy(f32[5,20,4,4,1,1]{1,3,5,4,2,0:T(4,128)S(1)} %collective-permute-done) | data formatting | bytes 12800 | tf_op jit(solution)/shard_map/ppermute | solution.py:22
  39.0 1.4 copy.792
  40.4 2.4 %pad_maximum_fusion = f32[5,20,4,4,1,130]{5,0,3,1,4,2:T(8,128)S(1)} fusion(f32[5,20,4,4,1,1]{5,0,3,1,4,2:T(8,128)S(1)} %copy.792, f32[5,20,1,4,1,128]{5,0,3,1,4,2:T(8,128)S(1)} %copy.1072, f32[5,20,1,4,1,128]{5,0,3,1,4,2:T(8,128)S(1)} %copy.1071, f32[5,20,1,4,1,128]{5,0,3,1,4,2:T(8,128)S(1)} %get-tuple-element.984, ...), kind=kLoop, calls=%fused_computation | loop fusion | flops 1040000 | bytes 1664000 | tf_op jit(solution)/shard_map/concatenate | solution.py:24
  43.5 3.2 %collective-permute-start.2 = (f32[5,20,4,4,1,130]{5,3,4,2,1,0:T(4,128)S(1)}, f32[5,20,4,4,1,130]{5,3,4,2,1,0:T(4,128)S(1)}, u32[]{:S(2)}, u32[]{:S(2)}) collective-permute-start(f32[5,20,4,4,1,130]{5,3,4,2,1,0:T(4,128)S(1)} %copy.793), channel_id=1, source_target_pairs={{0,4},{4,8},{8,12},{12,0},{1,5},{5,9},{9,13},{13,1},{2,6},{6,10},{... | collective-permute-start | bytes 2496008 | tf_op jit(solution)/shard_map/ppermute | solution.py:22
  46.7 3.6 %collective-permute-start.3 = (f32[5,20,4,4,1,130]{5,3,4,2,1,0:T(4,128)S(1)}, f32[5,20,4,4,1,130]{5,3,4,2,1,0:T(4,128)S(1)}, u32[]{:S(2)}, u32[]{:S(2)}) collective-permute-start(f32[5,20,4,4,1,130]{5,3,4,2,1,0:T(4,128)S(1)} %copy.793), channel_id=1, source_target_pairs={{4,0},{8,4},{12,8},{0,12},{5,1},{9,5},{13,9},{1,13},{6,2},{10,6},{... | collective-permute-start | bytes 2496008 | tf_op jit(solution)/shard_map/ppermute | solution.py:23
  52.6 27.9 %collective-permute-done.2 = f32[5,20,4,4,1,130]{5,3,4,2,1,0:T(4,128)S(1)} collective-permute-done((f32[5,20,4,4,1,130]{5,3,4,2,1,0:T(4,128)S(1)}, f32[5,20,4,4,1,130]{5,3,4,2,1,0:T(4,128)S(1)}, u32[]{:S(2)}, u32[]{:S(2)}) %collective-permute-start.2) | collective-permute-done | bytes 832032 | tf_op jit(solution)/shard_map/ppermute | solution.py:22
  81.4 2.3 %collective-permute-done.3 = f32[5,20,4,4,1,130]{5,3,4,2,1,0:T(4,128)S(1)} collective-permute-done((f32[5,20,4,4,1,130]{5,3,4,2,1,0:T(4,128)S(1)}, f32[5,20,4,4,1,130]{5,3,4,2,1,0:T(4,128)S(1)}, u32[]{:S(2)}, u32[]{:S(2)}) %collective-permute-start.3) | collective-permute-done | bytes 832032 | tf_op jit(solution)/shard_map/ppermute | solution.py:23
  88.1 2.3 %fusion.10 = f32[5,20,4,4,1,128]{5,3,2,1,0,4:T(4,128)S(1)} fusion(f32[5,20,4,4,1,128]{5,3,2,1,0,4:T(4,128)S(1)} %bitcast.7428, f32[4,4,1,1,1]{1,0,4,3,2:T(4,128)S(1)} %copy-done.22, f32[5,20,4,1,1,128]{5,3,2,1,0,4:T(1,128)S(1)} %copy.806, f32[5,20,4,1,1,128]{5,3,2,1,0,4:T(1,128)S(1)} %copy.805, f32[5,20,1,4,1,128]{5,3,2,1,0,4:T(4,128)S(1)} %copy.808, ...), kind=kOutput, calls=%fused_computation.18 | convolution fusion | flops 12083200 | bytes 4104272 | tf_op jit(solution)/shard_map/ci,fljiab->fljcab/dot_general | solution.py:68
  90.5 0.8 pad_maximum_fusion.11
  91.3 15.3 %all-to-all-start = ((f32[4,2,20,1,4,1,128]{6,4,2,1,5,3,0:T(4,128)}), f32[4,2,20,1,4,1,128]{6,4,2,1,5,3,0:T(4,128)S(1)}, u32[]{:S(2)}, u32[]{:S(2)}) async-start(f32[4,2,20,1,4,1,128]{6,4,2,1,5,3,0:T(4,128)} %pad_maximum_fusion.11), calls=%async_computation | async-start | bytes 655360 | tf_op jit(solution)/shard_map/all_to_all | solution.py:160
  106.9 14.1 %all-to-all-done = f32[4,2,20,1,4,1,128]{6,4,2,1,5,3,0:T(4,128)S(1)} async-done(((f32[4,2,20,1,4,1,128]{6,4,2,1,5,3,0:T(4,128)}), f32[4,2,20,1,4,1,128]{6,4,2,1,5,3,0:T(4,128)S(1)}, u32[]{:S(2)}, u32[]{:S(2)}) %all-to-all-start) | async-done | bytes 327712 | tf_op jit(solution)/shard_map/all_to_all | solution.py:160
  128.3 1.2 constant_dynamic-update-slice_fusion.79
  130.3 0.8 fusion.424
  131.9 0.8 fusion.410
  132.7 0.8 fusion.403
  133.4 0.8 fusion.396
  135.0 0.8 fusion.382
  135.8 0.8 fusion.375
  136.6 0.8 fusion.368
  137.3 0.8 fusion.361
  138.1 0.8 fusion.354
  138.9 0.8 fusion.347
  139.7 0.8 fusion.340
  140.5 0.8 fusion.333
  142.0 0.8 fusion.319
  142.8 0.8 fusion.312
  143.6 0.8 fusion.305
  144.4 1.0 bitcast_subtract_fusion.61
  145.4 1.3 bitcast_subtract_fusion.15
  147.4 1.2 multiply_subtract_fusion.37
  148.6 0.8 multiply_subtract_fusion.35
  151.0 0.8 pad_maximum_fusion.12
  151.8 10.4 %all-to-all-start.1 = ((f32[2,80,1,4,1,128]{5,3,4,2,0,1:T(4,128)}), f32[2,80,1,4,1,128]{5,3,4,2,0,1:T(4,128)S(1)}, u32[]{:S(2)}, u32[]{:S(2)}) async-start(f32[2,80,1,4,1,128]{5,3,4,2,0,1:T(4,128)} %pad_maximum_fusion.12), calls=%async_computation.1 | async-start | bytes 655360 | tf_op jit(solution)/shard_map/all_to_all | solution.py:171
  162.2 14.4 %all-to-all-done.1 = f32[2,80,1,4,1,128]{5,3,4,2,0,1:T(4,128)S(1)} async-done(((f32[2,80,1,4,1,128]{5,3,4,2,0,1:T(4,128)}), f32[2,80,1,4,1,128]{5,3,4,2,0,1:T(4,128)S(1)}, u32[]{:S(2)}, u32[]{:S(2)}) %all-to-all-start.1) | async-done | bytes 327712 | tf_op jit(solution)/shard_map/all_to_all | solution.py:171
  176.8 1.1 pad_maximum_fusion.2
  (218 shorter events, 23.0 us)
Async XLA Ops:
  0.0 29.9 %copy-start = (f32[5,5]{1,0:T(8,128)S(1)}, f32[5,5]{1,0:T(8,128)}, u32[]{:S(2)}) copy-start(f32[5,5]{1,0:T(8,128)} %param.12) | copy-start | bytes 304
  4.7 21.3 %copy-start.1 = (f32[5,20,4,4,1,128]{5,4,3,2,1,0:T(1,128)S(1)}, f32[5,20,4,4,1,128]{5,4,3,2,1,0:T(1,128)}, u32[]{:S(2)}) copy-start(f32[5,20,4,4,1,128]{5,4,3,2,1,0:T(1,128)} %param.9) | copy-start | bytes 2457604
  4.7 21.3 %copy-start.20 = (f32[5,5]{1,0:T(8,128)S(1)}, f32[5,5]{1,0:T(8,128)}, u32[]{:S(2)}) copy-start(f32[5,5]{1,0:T(8,128)} %param.11) | copy-start | bytes 304
  6.7 30.0 %collective-permute-start = (f32[5,20,4,4,1,1]{1,3,5,4,2,0:T(4,128)S(1)}, f32[5,20,4,4,1,1]{1,3,5,4,2,0:T(4,128)S(1)}, u32[]{:S(2)}, u32[]{:S(2)}) collective-permute-start(f32[5,20,4,4,1,1]{1,3,5,4,2,0:T(4,128)S(1)} %copy.789), channel_id=1, source_target_pairs={{0,16},{16,32},{32,48},{48,64},{64,80},{80,96},{96,112},{112,128},... | collective-permute-start | bytes 19208 | tf_op jit(solution)/shard_map/ppermute | solution.py:22
  12.4 26.6 %collective-permute-start.1 = (f32[5,20,4,4,1,1]{1,3,5,4,2,0:T(4,128)}, f32[5,20,4,4,1,1]{1,3,5,4,2,0:T(4,128)S(1)}, u32[]{:S(2)}, u32[]{:S(2)}) collective-permute-start(f32[5,20,4,4,1,1]{1,3,5,4,2,0:T(4,128)} %copy.790), channel_id=1, source_target_pairs={{16,0},{32,16},{48,32},{64,48},{80,64},{96,80},{112,96},{128,112},... | collective-permute-start | bytes 19208 | tf_op jit(solution)/shard_map/ppermute | solution.py:23
  27.7 1.7 copy-start.7
  27.7 1.7 copy-start.24
  31.7 0.9 copy-start.22
  31.7 3.8 %copy-start.25 = (s32[4,1,128]{2,1,0:T(1,128)S(1)}, s32[4,1,128]{2,1,0:T(1,128)}, u32[]{:S(2)}) copy-start(s32[4,1,128]{2,1,0:T(1,128)} %param.14) | copy-start | bytes 6148
  42.8 7.5 %copy-start.2 = (f32[5,20,4,4,1,1]{5,0,3,1,4,2:T(8,128)S(1)}, f32[5,20,4,4,1,1]{5,0,3,1,4,2:T(8,128)}, u32[]{:S(2)}) copy-start(f32[5,20,4,4,1,1]{5,0,3,1,4,2:T(8,128)} %copy.791) | copy-start | bytes 19204
  42.8 7.5 %copy-start.23 = (pred[128]{0:T(512)(128)(4,1)S(1)}, pred[128]{0:T(512)(128)(4,1)}, u32[]{:S(2)}) copy-start(pred[128]{0:T(512)(128)(4,1)} %get-tuple-element.982) | copy-start | bytes 388
  43.5 37.0 %collective-permute-start.2 = (f32[5,20,4,4,1,130]{5,3,4,2,1,0:T(4,128)S(1)}, f32[5,20,4,4,1,130]{5,3,4,2,1,0:T(4,128)S(1)}, u32[]{:S(2)}, u32[]{:S(2)}) collective-permute-start(f32[5,20,4,4,1,130]{5,3,4,2,1,0:T(4,128)S(1)} %copy.793), channel_id=1, source_target_pairs={{0,4},{4,8},{8,12},{12,0},{1,5},{5,9},{9,13},{13,1},{2,6},{6,10},{... | collective-permute-start | bytes 2496008 | tf_op jit(solution)/shard_map/ppermute | solution.py:22
  46.7 36.9 %collective-permute-start.3 = (f32[5,20,4,4,1,130]{5,3,4,2,1,0:T(4,128)S(1)}, f32[5,20,4,4,1,130]{5,3,4,2,1,0:T(4,128)S(1)}, u32[]{:S(2)}, u32[]{:S(2)}) collective-permute-start(f32[5,20,4,4,1,130]{5,3,4,2,1,0:T(4,128)S(1)} %copy.793), channel_id=1, source_target_pairs={{4,0},{8,4},{12,8},{0,12},{5,1},{9,5},{13,9},{1,13},{6,2},{10,6},{... | collective-permute-start | bytes 2496008 | tf_op jit(solution)/shard_map/ppermute | solution.py:23
  50.3 0.6 copy-start.29
  51.0 0.8 copy-start.28
  52.5 28.8 %copy-start.27 = (pred[128]{0:T(512)(128)(4,1)S(1)}, pred[128]{0:T(512)(128)(4,1)}, u32[]{:S(2)}) copy-start(pred[128]{0:T(512)(128)(4,1)} %get-tuple-element.963) | copy-start | bytes 388
  81.4 3.1 %copy-start.26 = (pred[128]{0:T(512)(128)(4,1)S(1)}, pred[128]{0:T(512)(128)(4,1)}, u32[]{:S(2)}) copy-start(pred[128]{0:T(512)(128)(4,1)} %get-tuple-element.964) | copy-start | bytes 388
  84.5 1.0 copy-start.15
  84.5 1.1 copy-start.16
  84.5 1.2 copy-start.17
  84.5 1.2 copy-start.18
  86.6 1.3 copy-start.8
  86.6 1.5 copy-start.19
  86.6 1.5 copy-start.30
  86.6 1.5 copy-start.31
  90.4 16.2 %copy-start.9 = (f32[4,80,1,4,1,128]{5,4,3,2,1,0:T(1,128)S(1)}, f32[4,80,1,4,1,128]{5,4,3,2,1,0:T(1,128)}, u32[]{:S(2)}) copy-start(f32[4,80,1,4,1,128]{5,4,3,2,1,0:T(1,128)} %param.15) | copy-start | bytes 1966084
  90.4 16.1 %copy-start.21 = (f32[1,4,1,128]{3,2,1,0:T(1,128)S(1)}, f32[1,4,1,128]{3,2,1,0:T(1,128)}, u32[]{:S(2)}) copy-start(f32[1,4,1,128]{3,2,1,0:T(1,128)} %param.16) | copy-start | bytes 6148
  91.3 29.7 %all-to-all-start = ((f32[4,2,20,1,4,1,128]{6,4,2,1,5,3,0:T(4,128)}), f32[4,2,20,1,4,1,128]{6,4,2,1,5,3,0:T(4,128)S(1)}, u32[]{:S(2)}, u32[]{:S(2)}) async-start(f32[4,2,20,1,4,1,128]{6,4,2,1,5,3,0:T(4,128)} %pad_maximum_fusion.11), calls=%async_computation | async-start | bytes 655360 | tf_op jit(solution)/shard_map/all_to_all | solution.py:160
  106.7 22.9 %copy-start.14 = (f32[80,1,4,1,128]{4,2,3,1,0:T(4,128)}, f32[80,1,4,1,128]{4,2,3,1,0:T(4,128)S(1)}, u32[]{:S(2)}) copy-start(f32[80,1,4,1,128]{4,2,3,1,0:T(4,128)S(1)} %bitcast_add_fusion) | copy-start | bytes 491524
  106.8 15.7 %copy-start.3 = (f32[1,80,1,4,1,128]{5,3,4,2,1,0:T(4,128)}, f32[1,80,1,4,1,128]{5,3,4,2,1,0:T(4,128)S(1)}, u32[]{:S(2)}) copy-start(f32[1,80,1,4,1,128]{5,3,4,2,1,0:T(4,128)S(1)} %get-tuple-element.716) | copy-start | bytes 491524
  106.9 22.7 %copy-start.5 = (f32[1,80,1,4,1,128]{5,3,4,2,1,0:T(4,128)}, f32[1,80,1,4,1,128]{5,3,4,2,1,0:T(4,128)S(1)}, u32[]{:S(2)}) copy-start(f32[1,80,1,4,1,128]{5,3,4,2,1,0:T(4,128)S(1)} %get-tuple-element.719) | copy-start | bytes 491524
  106.9 22.7 %copy-start.10 = (f32[1,80,1,4,1,128]{5,3,4,2,1,0:T(4,128)}, f32[1,80,1,4,1,128]{5,3,4,2,1,0:T(4,128)S(1)}, u32[]{:S(2)}) copy-start(f32[1,80,1,4,1,128]{5,3,4,2,1,0:T(4,128)S(1)} %get-tuple-element.718) | copy-start | bytes 491524
  106.9 22.7 %copy-start.13 = (f32[1,80,1,4,1,128]{5,3,4,2,1,0:T(4,128)}, f32[1,80,1,4,1,128]{5,3,4,2,1,0:T(4,128)S(1)}, u32[]{:S(2)}) copy-start(f32[1,80,1,4,1,128]{5,3,4,2,1,0:T(4,128)S(1)} %get-tuple-element.717) | copy-start | bytes 491524
  121.2 8.3 %copy-start.11 = (f32[80,1,4,1,128]{4,2,3,1,0:T(4,128)}, f32[80,1,4,1,128]{4,2,3,1,0:T(4,128)S(1)}, u32[]{:S(2)}) copy-start(f32[80,1,4,1,128]{4,2,3,1,0:T(4,128)S(1)} %multiply_subtract_fusion) | copy-start | bytes 491524
  122.6 21.8 %copy-start.4 = (f32[1,80,1,4,1,128]{5,3,4,2,1,0:T(4,128)S(1)}, f32[1,80,1,4,1,128]{5,3,4,2,1,0:T(4,128)}, u32[]{:S(2)}) copy-start(f32[1,80,1,4,1,128]{5,3,4,2,1,0:T(4,128)} %copy-done.3) | copy-start | bytes 491524
  130.2 15.1 %copy-start.6 = (f32[1,80,1,4,1,128]{5,3,4,2,1,0:T(4,128)S(1)}, f32[1,80,1,4,1,128]{5,3,4,2,1,0:T(4,128)}, u32[]{:S(2)}) copy-start(f32[1,80,1,4,1,128]{5,3,4,2,1,0:T(4,128)} %copy-done.5) | copy-start | bytes 491524
  130.3 17.2 %copy-start.12 = (f32[80,1,4,1,128]{4,2,3,1,0:T(4,128)S(1)}, f32[80,1,4,1,128]{4,2,3,1,0:T(4,128)}, u32[]{:S(2)}) copy-start(f32[80,1,4,1,128]{4,2,3,1,0:T(4,128)} %copy-done.11) | copy-start | bytes 491524
  151.8 24.8 %all-to-all-start.1 = ((f32[2,80,1,4,1,128]{5,3,4,2,0,1:T(4,128)}), f32[2,80,1,4,1,128]{5,3,4,2,0,1:T(4,128)S(1)}, u32[]{:S(2)}, u32[]{:S(2)}) async-start(f32[2,80,1,4,1,128]{5,3,4,2,0,1:T(4,128)} %pad_maximum_fusion.12), calls=%async_computation.1 | async-start | bytes 655360 | tf_op jit(solution)/shard_map/all_to_all | solution.py:171
